TPU v7x, 32 devices: a whole 2x2x4 slice. The times are simulated.
32 devices in a mesh: groups: 2 (over y), row: 4 (over z), col: 4 (over x, core).
Axes of the slice: x: 2, y: 2, z: 4, core: 2. Of those that a mesh axis runs over, the one named last changes fastest.
Arguments:
- factor_blocks: bfloat16 [20, 4096, 4096], P('groups', 'row', 'col'), parts along dimension 0, may hold values from -0.0390625 to 0.0390625
- inverse_blocks: bfloat16 [10, 4096, 4096], P('groups', 'col', 'row'), parts along dimension 0, as said below
- right_sides: bfloat16 [10, 4096, 256], P('groups', 'row'), parts along dimension 0, may hold values from -6 to 6
Outputs:
- solution: bfloat16 [10, 4096, 256], P('groups', 'col', 'row'), parts along dimension 0
There are 2 independent parts, one for each index of `groups`. A program takes and returns all parts, laid end to end along the dimension named above; each array names one. Nothing has to cross between parts.
Inputs may be any that keep to these rules, and one draw needn't show every extreme that they name: `inverse_blocks`: each block is lower triangular with a diagonal of 0.5 to 2, hence invertible.
All inputs are finite; a program needn't handle non-finite values.
Results may differ from a plain program's by a relative error of at most 0.0095.
Values may be sent and summed in bfloat16 or wider, within the bound.
A program may use at most 64 MiB of HBM per device.

v0:
```python
import jax
import jax.numpy as jnp
from jax import lax
from jax.sharding import PartitionSpec as P


def pair_index(block_row, column_index):
    return block_row * (block_row - 1) // 2 + column_index


def per_device(factor_blocks, inverse_blocks, right_sides):
    steps_total = right_sides.shape[0]
    angles = right_sides.shape[2]
    col_rows = inverse_blocks.shape[1]
    solved = []
    outputs = []
    for block_row in range(steps_total):
        residual = right_sides[block_row].astype(jnp.float32)
        if block_row > 0:
            partial_value = jnp.zeros((right_sides.shape[1], angles), jnp.float32)
            for column_index in range(block_row):
                partial_value = partial_value + jnp.dot(
                    factor_blocks[pair_index(block_row, column_index)],
                    solved[column_index],
                    preferred_element_type=jnp.float32,
                )
            residual = residual - lax.psum(partial_value, "col")
        residual_bf = residual.astype(jnp.bfloat16)
        term = jnp.dot(inverse_blocks[block_row], residual_bf, preferred_element_type=jnp.float32)
        share = lax.psum_scatter(term, "row", scatter_dimension=1, tiled=True).astype(jnp.bfloat16)
        outputs.append(share)
        if block_row + 1 < steps_total:
            current = lax.all_gather(share, "row", axis=1, tiled=True)
        else:
            current = jnp.zeros((col_rows, angles), jnp.bfloat16)
        solved.append(current)
    return jnp.stack(outputs, axis=0)


def solution(mesh):
    placed = (P("groups", "row", "col"), P("groups", "col", "row"), P("groups", "row", None))
    return jax.shard_map(
        per_device, mesh=mesh, in_specs=placed, out_specs=P("groups", "col", "row"), check_vma=False
    )
```

profile of v0, /device:TPU:0, one launch (start us, length us, event | category | flops | bytes accessed | tf_op | source)
XLA Modules:
  0.0 406.6 jit_solution(15479284260959443623)
XLA Ops:
  6.5 3.4 fusion.28
  9.9 0.0 reduce-scatter.6.cloned.1.call-update
  10.0 0.0 all-reduce.5.cloned.1.call-start
  10.0 30.1 %reduce-scatter.6.cloned.1.call-done = f32[1024,64]{0,1:T(8,128)} async-done(((f32[1024,256]{0,1:T(8,128)}), f32[1024,64]{0,1:T(8,128)}) %reduce-scatter.6.cloned.1.call-update) | async-done | bytes 262160 | tf_op jit(solution)/shard_map/reduce_scatter | solution.py:30
  40.1 1.6 bitcast_dynamic-update-slice_fusion.4
  41.8 15.9 %all_gather.12 = bf16[1024,256]{0,1:T(8,128)(2,1)S(1)} all-gather(bf16[1024,64]{0,1:T(8,128)(2,1)S(1)} %get-tuple-element.12), channel_id=1, replica_groups=mesh['groups'=2,'row'=4,'col'=4] {'row'}, dimensions={1}, use_global_device_ids=true | all-gather | bytes 655360 | tf_op jit(solution)/shard_map/all_gather | solution.py:33
  57.7 3.5 fusion.45
  61.2 0.0 all-reduce.5.cloned.1.call-update
  61.2 0.0 reduce-scatter.8.cloned.1.call-start
  61.3 34.7 %all-reduce.5.cloned.1.call-done = f32[1024,256]{1,0:T(8,128)} async-done(((f32[1024,256]{1,0:T(8,128)}), f32[1024,256]{1,0:T(8,128)}) %all-reduce.5.cloned.1.call-update) | async-done | bytes 1048592 | tf_op jit(solution)/shard_map/psum | solution.py:27
  96.0 3.7 fusion.48
  99.7 0.0 reduce-scatter.8.cloned.1.call-update
  99.7 0.0 all-reduce.7.cloned.1.call-start
  99.8 27.9 %reduce-scatter.8.cloned.1.call-done = f32[1024,64]{0,1:T(8,128)} async-done(((f32[1024,256]{0,1:T(8,128)}), f32[1024,64]{0,1:T(8,128)}) %reduce-scatter.8.cloned.1.call-update) | async-done | bytes 262160 | tf_op jit(solution)/shard_map/reduce_scatter | solution.py:30
  127.6 1.6 bitcast_dynamic-update-slice_fusion.3
  129.3 16.0 %all_gather.13 = bf16[1024,256]{0,1:T(8,128)(2,1)S(1)} all-gather(bf16[1024,64]{0,1:T(8,128)(2,1)S(1)} %get-tuple-element.10), channel_id=1, replica_groups=mesh['groups'=2,'row'=4,'col'=4] {'row'}, dimensions={1}, use_global_device_ids=true | all-gather | bytes 655360 | tf_op jit(solution)/shard_map/all_gather | solution.py:33
  145.2 0.8 copy-done.4
  146.0 2.3 fusion.20
  148.4 3.3 fusion.63
  151.7 0.0 all-reduce.7.cloned.1.call-update
  151.7 0.0 reduce-scatter.10.cloned.1.call-start
  151.8 34.7 %all-reduce.7.cloned.1.call-done = f32[1024,256]{1,0:T(8,128)} async-done(((f32[1024,256]{1,0:T(8,128)}), f32[1024,256]{1,0:T(8,128)}) %all-reduce.7.cloned.1.call-update) | async-done | bytes 1048592 | tf_op jit(solution)/shard_map/psum | solution.py:27
  186.5 3.6 fusion.51
  190.1 0.0 reduce-scatter.10.cloned.1.call-update
  190.1 0.0 all-reduce.9.cloned.1.call-start
  190.2 3.5 fusion.14
  193.7 24.4 %reduce-scatter.10.cloned.1.call-done = f32[1024,64]{0,1:T(8,128)} async-done(((f32[1024,256]{0,1:T(8,128)}), f32[1024,64]{0,1:T(8,128)}) %reduce-scatter.10.cloned.1.call-update) | async-done | bytes 262160 | tf_op jit(solution)/shard_map/reduce_scatter | solution.py:30
  218.0 1.7 bitcast_dynamic-update-slice_fusion.2
  219.8 16.0 %all_gather.14 = bf16[1024,256]{0,1:T(8,128)(2,1)S(1)} all-gather(bf16[1024,64]{0,1:T(8,128)(2,1)S(1)} %get-tuple-element.8), channel_id=1, replica_groups=mesh['groups'=2,'row'=4,'col'=4] {'row'}, dimensions={1}, use_global_device_ids=true | all-gather | bytes 655360 | tf_op jit(solution)/shard_map/all_gather | solution.py:33
  235.7 0.8 copy-done.5
  236.5 2.3 fusion.12
  238.9 3.3 fusion.72
  242.2 0.0 reduce-scatter.12.cloned.1.call-start
  242.3 34.7 %all-reduce.9.cloned.1.call-done = f32[1024,256]{1,0:T(8,128)} async-done(((f32[1024,256]{1,0:T(8,128)}), f32[1024,256]{1,0:T(8,128)}) %all-reduce.9.cloned.1.call-update) | async-done | bytes 1048592 | tf_op jit(solution)/shard_map/psum | solution.py:27
  277.0 3.6 fusion.54
  280.6 0.0 all-reduce.11.cloned.1.call-start
  280.7 3.6 fusion.6
  284.3 3.3 fusion.4
  287.6 21.0 %reduce-scatter.12.cloned.1.call-done = f32[1024,64]{0,1:T(8,128)} async-done(((f32[1024,256]{0,1:T(8,128)}), f32[1024,64]{0,1:T(8,128)}) %reduce-scatter.12.cloned.1.call-update) | async-done | bytes 262160 | tf_op jit(solution)/shard_map/reduce_scatter | solution.py:30
  308.6 1.8 bitcast_dynamic-update-slice_fusion.1
  310.3 15.9 %all_gather.15 = bf16[1024,256]{0,1:T(8,128)(2,1)S(1)} all-gather(bf16[1024,64]{0,1:T(8,128)(2,1)S(1)} %get-tuple-element.6), channel_id=1, replica_groups=mesh['groups'=2,'row'=4,'col'=4] {'row'}, dimensions={1}, use_global_device_ids=true | all-gather | bytes 655360 | tf_op jit(solution)/shard_map/all_gather | solution.py:33
  326.2 2.3 fusion.2
  328.6 3.4 fusion.84
  332.0 0.0 reduce-scatter.14.cloned.1.call-start
  332.1 34.8 %all-reduce.11.cloned.1.call-done = f32[1024,256]{1,0:T(8,128)} async-done(((f32[1024,256]{1,0:T(8,128)}), f32[1024,256]{1,0:T(8,128)}) %all-reduce.11.cloned.1.call-update) | async-done | bytes 1048592 | tf_op jit(solution)/shard_map/psum | solution.py:27
  366.8 3.7 fusion.57
  370.5 27.9 %reduce-scatter.14.cloned.1.call-done = f32[1024,64]{0,1:T(8,128)} async-done(((f32[1024,256]{0,1:T(8,128)}), f32[1024,64]{0,1:T(8,128)}) %reduce-scatter.14.cloned.1.call-update) | async-done | bytes 262160 | tf_op jit(solution)/shard_map/reduce_scatter | solution.py:30
  398.4 1.6 bitcast_dynamic-update-slice_fusion
  (17 shorter events, 0.1 us)
Async XLA Ops:
  6.5 33.6 %reduce-scatter.6.cloned.1.call-start = ((), (), s32[]{:S(2)}) async-start(), calls=%async_computation.5 | async-start | bytes 1310720 | tf_op jit(solution)/shard_map/reduce_scatter | solution.py:30
  10.0 86.0 %all-reduce.5.cloned.1.call-start = ((), (), s32[]{:S(2)}) async-start(), calls=%async_computation.6 | async-start | bytes 2097152 | tf_op jit(solution)/shard_map/psum | solution.py:27
  57.7 38.3 %copy-start = (bf16[5,1024,256]{2,1,0:T(8,128)(2,1)S(1)}, bf16[5,1024,256]{2,1,0:T(8,128)(2,1)}, u32[]{:S(2)}) copy-start(bf16[5,1024,256]{2,1,0:T(8,128)(2,1)} %param.5) | copy-start | bytes 7864324
  61.2 66.4 %reduce-scatter.8.cloned.1.call-start = ((), (), s32[]{:S(2)}) async-start(), calls=%async_computation.7 | async-start | bytes 1310720 | tf_op jit(solution)/shard_map/reduce_scatter | solution.py:30
  99.7 86.7 %all-reduce.7.cloned.1.call-start = ((), (), s32[]{:S(2)}) async-start(), calls=%async_computation.8 | async-start | bytes 2097152 | tf_op jit(solution)/shard_map/psum | solution.py:27
  145.2 0.8 copy-start.4
  151.7 66.3 %reduce-scatter.10.cloned.1.call-start = ((), (), s32[]{:S(2)}) async-start(), calls=%async_computation.9 | async-start | bytes 1310720 | tf_op jit(solution)/shard_map/reduce_scatter | solution.py:30
  190.1 86.8 %all-reduce.9.cloned.1.call-start = ((), (), s32[]{:S(2)}) async-start(), calls=%async_computation.10 | async-start | bytes 2097152 | tf_op jit(solution)/shard_map/psum | solution.py:27
  218.0 20.8 %copy-start.3 = (f32[256,1024]{0,1:T(8,128)S(1)}, f32[256,1024]{0,1:T(8,128)}, u32[]{:S(2)}) copy-start(f32[256,1024]{0,1:T(8,128)} %fusion.14) | copy-start | bytes 3145732
  235.7 0.8 copy-start.5
  242.2 66.3 %reduce-scatter.12.cloned.1.call-start = ((), (), s32[]{:S(2)}) async-start(), calls=%async_computation.11 | async-start | bytes 1310720 | tf_op jit(solution)/shard_map/reduce_scatter | solution.py:30
  280.6 86.2 %all-reduce.11.cloned.1.call-start = ((), (), s32[]{:S(2)}) async-start(), calls=%async_computation.12 | async-start | bytes 2097152 | tf_op jit(solution)/shard_map/psum | solution.py:27
  280.7 3.6 copy-start.6
  308.6 20.0 %copy-start.1 = (f32[256,1024]{0,1:T(8,128)S(1)}, f32[256,1024]{0,1:T(8,128)}, u32[]{:S(2)}) copy-start(f32[256,1024]{0,1:T(8,128)} %fusion.6) | copy-start | bytes 3145732
  308.6 20.0 %copy-start.2 = (f32[256,1024]{0,1:T(8,128)S(1)}, f32[256,1024]{0,1:T(8,128)}, u32[]{:S(2)}) copy-start(f32[256,1024]{0,1:T(8,128)} %fusion.4) | copy-start | bytes 3145732
  332.0 66.4 %reduce-scatter.14.cloned.1.call-start = ((), (), s32[]{:S(2)}) async-start(), calls=%async_computation.13 | async-start | bytes 1310720 | tf_op jit(solution)/shard_map/reduce_scatter | solution.py:30
Sparse Core Ops, SparseCore 0:
  10.1 29.9 reduce-scatter.5
  61.3 34.6 all-reduce.4
  99.8 27.7 reduce-scatter.7
  151.8 34.5 all-reduce.6
  190.2 27.7 reduce-scatter.9
  242.3 34.5 all-reduce.8
  280.8 27.7 reduce-scatter.11
  332.1 34.6 all-reduce.10
  370.6 27.7 reduce-scatter.13
where the time goes:
time: 407 us
  waiting for transfers between devices  270 us (66%)
  blocking collectives  63.8 us (16%)
  matrix products  49 us (12%)
  between operations  13.3 us (3%)
  other arithmetic  8.36 us (2%)
    psum x4, waiting for transfers between devices, per_device(): residual = residual - lax.psum(partial_value, 'col')  139 us
    reduce_scatter x5, waiting for transfers between devices, per_device(): lax.psum_scatter(term, 'row', scatter_dimension=1, tiled=True)  131 us
    all_gather x4, blocking collectives, per_device(): current = lax.all_gather(share, 'row', axis=1, tiled=True)  63.8 us
    dot_general x10, matrix products, per_device(): jnp.dot(factor_blocks[pair_index(block_row, column_index)], solved[column...  30.9 us
    dot_general x5, matrix products, per_device(): jnp.dot(inverse_blocks[block_row], residual_bf, preferred_element_type=jn...  18.1 us
  transfers between devices with their start and end apart: 9, of which 9 were waited for; matrix products, arithmetic and copies ran while one was open for 3% of the time, Pallas kernels for 0%

commit v1 on v0

--- a/solution.py
+++ b/solution.py
@@ -24,7 +24,7 @@
                     solved[column_index],
                     preferred_element_type=jnp.float32,
                 )
-            residual = residual - lax.psum(partial_value, "col")
+            residual = residual - jnp.sum(lax.all_gather(partial_value, "col"), axis=0)
         residual_bf = residual.astype(jnp.bfloat16)
         term = jnp.dot(inverse_blocks[block_row], residual_bf, preferred_element_type=jnp.float32)
         share = lax.psum_scatter(term, "row", scatter_dimension=1, tiled=True).astype(jnp.bfloat16)

time: 407 us -> 440 us (1.081)
  local copies, waits for them, and re-layouts: 1.62 us -> 28.4 us
  other arithmetic: 8.36 us -> 27.2 us
  waiting for transfers between devices: 270 us -> 260 us
    psum x4 -> x0, waiting for transfers between devices: 139 us -> none  [per_device(): residual = residual - lax.psum(partial_value, 'col')]
    all_gather x0 -> x4, waiting for transfers between devices: none -> 128 us  [per_device(): residual = residual - jnp.sum(lax.all_gather(partial_value, 'col'), axis=0)]
    all_gather x0 -> x4, local copies, waits for them, and re-layouts: none -> 24.2 us  [per_device(): residual = residual - jnp.sum(lax.all_gather(partial_value, 'col'), axis=0)]
    reduce_sum x0 -> x4, other arithmetic: none -> 19 us  [per_device(): residual = residual - jnp.sum(lax.all_gather(partial_value, 'col'), axis=0)]
where the time goes in v1:
time: 440 us; the launch traced here: 439 us
  waiting for transfers between devices  260 us (59%)
  blocking collectives  63.8 us (14%)
  matrix products  45.5 us (10%)
  local copies, waits for them, and re-layouts  28.4 us (6%)
  other arithmetic  27.2 us (6%)
  between operations  13.3 us (3%)
    reduce_scatter x5, waiting for transfers between devices, per_device(): lax.psum_scatter(term, 'row', scatter_dimension=1, tiled=True)  131 us
    all_gather x4, waiting for transfers between devices, per_device(): residual = residual - jnp.sum(lax.all_gather(partial_value, 'col'), axis=0)  128 us
    all_gather x4, blocking collectives, per_device(): current = lax.all_gather(share, 'row', axis=1, tiled=True)  63.8 us
    dot_general x10, matrix products, per_device(): jnp.dot(factor_blocks[pair_index(block_row, column_index)], solved[column...  28.8 us
    all_gather x4, local copies, waits for them, and re-layouts, per_device(): residual = residual - jnp.sum(lax.all_gather(partial_value, 'col'), axis=0)  24.2 us
    reduce_sum x4, other arithmetic, per_device(): residual = residual - jnp.sum(lax.all_gather(partial_value, 'col'), axis=0)  19 us
    dot_general x5, matrix products, per_device(): jnp.dot(inverse_blocks[block_row], residual_bf, preferred_element_type=jn...  16.7 us
  transfers between devices with their start and end apart: 9, of which 9 were waited for; matrix products, arithmetic and copies ran while one was open for 3% of the time, Pallas kernels for 0%

profile of v1, /device:TPU:0, one launch (start us, length us, event | category | flops | bytes accessed | tf_op | source)
XLA Modules:
  0.0 438.5 jit_solution(7066276382499517516)
XLA Ops:
  6.5 3.4 fusion.28
  10.0 30.1 %reduce-scatter.6.cloned.1.call-done = f32[1024,64]{0,1:T(8,128)} async-done(((f32[1024,256]{0,1:T(8,128)}), f32[1024,64]{0,1:T(8,128)}) %reduce-scatter.6.cloned.1.call-update) | async-done | bytes 262160 | tf_op jit(solution)/shard_map/reduce_scatter | solution.py:30
  40.1 1.6 bitcast_dynamic-update-slice_fusion.4
  41.7 16.0 %all_gather.36 = bf16[1024,256]{0,1:T(8,128)(2,1)S(1)} all-gather(bf16[1024,64]{0,1:T(8,128)(2,1)S(1)} %get-tuple-element.12), channel_id=1, replica_groups=mesh['groups'=2,'row'=4,'col'=4] {'row'}, dimensions={1}, use_global_device_ids=true | all-gather | bytes 655360 | tf_op jit(solution)/shard_map/all_gather | solution.py:33
  57.7 3.3 fusion.45
  61.1 2.5 fusion.101
  63.8 30.2 %all-gather.9.cloned.1.call-done = f32[4096,256]{0,1:T(8,128)} async-done(((f32[1024,256]{0,1:T(8,128)}), f32[4096,256]{0,1:T(8,128)}) %all-gather.9.cloned.1.call-update) | async-done | bytes 4194320 | tf_op jit(solution)/shard_map/all_gather | solution.py:27
  94.0 6.1 %reshape.8 = f32[4,1024,256]{1,0,2:T(4,128)} reshape(f32[4096,256]{0,1:T(8,128)} %all-gather.9.cloned.1.call-done) | data formatting | bytes 8388608 | tf_op jit(solution)/shard_map/all_gather | solution.py:27
  100.0 4.7 %reduce_sum.44 = f32[1024,256]{0,1:T(8,128)S(1)} reduce(f32[4,1024,256]{1,0,2:T(4,128)} %reshape.8, f32[]{:T(128)} %constant.0.clone.1), dimensions={0}, to_apply=%region_1.0 | reduce | flops 786432 | bytes 5242884 | tf_op jit(solution)/shard_map/reduce_sum | solution.py:27
  104.8 3.3 fusion.48
  108.2 27.4 %reduce-scatter.8.cloned.1.call-done = f32[1024,64]{0,1:T(8,128)} async-done(((f32[1024,256]{0,1:T(8,128)}), f32[1024,64]{0,1:T(8,128)}) %reduce-scatter.8.cloned.1.call-update) | async-done | bytes 262160 | tf_op jit(solution)/shard_map/reduce_scatter | solution.py:30
  135.6 1.6 bitcast_dynamic-update-slice_fusion.3
  137.2 16.0 %all_gather.39 = bf16[1024,256]{0,1:T(8,128)(2,1)S(1)} all-gather(bf16[1024,64]{0,1:T(8,128)(2,1)S(1)} %get-tuple-element.10), channel_id=1, replica_groups=mesh['groups'=2,'row'=4,'col'=4] {'row'}, dimensions={1}, use_global_device_ids=true | all-gather | bytes 655360 | tf_op jit(solution)/shard_map/all_gather | solution.py:33
  153.2 0.8 copy-done.2
  154.0 2.4 fusion.20
  156.4 3.3 fusion.63
  159.7 0.2 reduce-scatter.10.cloned.1.call-start
  159.9 0.2 copy.9
  160.2 32.5 %all-gather.11.cloned.1.call-done = f32[4096,256]{0,1:T(8,128)} async-done(((f32[1024,256]{0,1:T(8,128)}), f32[4096,256]{0,1:T(8,128)}) %all-gather.11.cloned.1.call-update) | async-done | bytes 4194320 | tf_op jit(solution)/shard_map/all_gather | solution.py:27
  192.7 6.1 %reshape.9 = f32[4,1024,256]{1,0,2:T(4,128)} reshape(f32[4096,256]{0,1:T(8,128)} %all-gather.11.cloned.1.call-done) | data formatting | bytes 8388608 | tf_op jit(solution)/shard_map/all_gather | solution.py:27
  198.7 4.7 %reduce_sum.46 = f32[1024,256]{0,1:T(8,128)S(1)} reduce(f32[4,1024,256]{1,0,2:T(4,128)} %reshape.9, f32[]{:T(128)} %constant.0.clone.1), dimensions={0}, to_apply=%region_3.0 | reduce | flops 786432 | bytes 5242884 | tf_op jit(solution)/shard_map/reduce_sum | solution.py:27
  203.5 3.3 fusion.51
  206.9 2.5 fusion.14
  209.4 24.9 %reduce-scatter.10.cloned.1.call-done = f32[1024,64]{0,1:T(8,128)} async-done(((f32[1024,256]{0,1:T(8,128)}), f32[1024,64]{0,1:T(8,128)}) %reduce-scatter.10.cloned.1.call-update) | async-done | bytes 262160 | tf_op jit(solution)/shard_map/reduce_scatter | solution.py:30
  234.3 1.6 bitcast_dynamic-update-slice_fusion.2
  235.9 16.0 %all_gather.42 = bf16[1024,256]{0,1:T(8,128)(2,1)S(1)} all-gather(bf16[1024,64]{0,1:T(8,128)(2,1)S(1)} %get-tuple-element.8), channel_id=1, replica_groups=mesh['groups'=2,'row'=4,'col'=4] {'row'}, dimensions={1}, use_global_device_ids=true | all-gather | bytes 655360 | tf_op jit(solution)/shard_map/all_gather | solution.py:33
  251.9 2.5 fusion.12
  254.4 3.3 fusion.72
  257.8 0.2 copy.10
  258.0 32.7 %all-gather.13.cloned.1.call-done = f32[4096,256]{0,1:T(8,128)} async-done(((f32[1024,256]{0,1:T(8,128)}), f32[4096,256]{0,1:T(8,128)}) %all-gather.13.cloned.1.call-update) | async-done | bytes 4194320 | tf_op jit(solution)/shard_map/all_gather | solution.py:27
  290.7 6.1 %reshape.10 = f32[4,1024,256]{1,0,2:T(4,128)} reshape(f32[4096,256]{0,1:T(8,128)} %all-gather.13.cloned.1.call-done) | data formatting | bytes 8388608 | tf_op jit(solution)/shard_map/all_gather | solution.py:27
  296.8 4.7 %reduce_sum.48 = f32[1024,256]{0,1:T(8,128)S(1)} reduce(f32[4,1024,256]{1,0,2:T(4,128)} %reshape.10, f32[]{:T(128)} %constant.0.clone.1), dimensions={0}, to_apply=%region_5.0 | reduce | flops 786432 | bytes 5242884 | tf_op jit(solution)/shard_map/reduce_sum | solution.py:27
  301.5 3.4 fusion.54
  304.9 0.3 all-gather.15.cloned.1.call-start
  305.2 2.3 fusion.6
  307.6 3.3 fusion.4
  310.9 21.5 %reduce-scatter.12.cloned.1.call-done = f32[1024,64]{0,1:T(8,128)} async-done(((f32[1024,256]{0,1:T(8,128)}), f32[1024,64]{0,1:T(8,128)}) %reduce-scatter.12.cloned.1.call-update) | async-done | bytes 262160 | tf_op jit(solution)/shard_map/reduce_scatter | solution.py:30
  332.4 1.7 bitcast_dynamic-update-slice_fusion.1
  334.1 16.0 %all_gather.45 = bf16[1024,256]{0,1:T(8,128)(2,1)S(1)} all-gather(bf16[1024,64]{0,1:T(8,128)(2,1)S(1)} %get-tuple-element.6), channel_id=1, replica_groups=mesh['groups'=2,'row'=4,'col'=4] {'row'}, dimensions={1}, use_global_device_ids=true | all-gather | bytes 655360 | tf_op jit(solution)/shard_map/all_gather | solution.py:33
  350.1 2.3 fusion.2
  352.4 3.4 fusion.84
  355.9 0.2 copy.11
  356.1 32.7 %all-gather.15.cloned.1.call-done = f32[4096,256]{0,1:T(8,128)} async-done(((f32[1024,256]{0,1:T(8,128)}), f32[4096,256]{0,1:T(8,128)}) %all-gather.15.cloned.1.call-update) | async-done | bytes 4194320 | tf_op jit(solution)/shard_map/all_gather | solution.py:27
  388.8 6.1 %reshape.11 = f32[4,1024,256]{1,0,2:T(4,128)} reshape(f32[4096,256]{0,1:T(8,128)} %all-gather.15.cloned.1.call-done) | data formatting | bytes 8388608 | tf_op jit(solution)/shard_map/all_gather | solution.py:27
  394.8 4.7 %reduce_sum.50 = f32[1024,256]{0,1:T(8,128)S(1)} reduce(f32[4,1024,256]{1,0,2:T(4,128)} %reshape.11, f32[]{:T(128)} %constant.0.clone.1), dimensions={0}, to_apply=%region_7.0 | reduce | flops 786432 | bytes 5242884 | tf_op jit(solution)/shard_map/reduce_sum | solution.py:27
  399.6 3.3 fusion.57
  402.9 27.4 %reduce-scatter.14.cloned.1.call-done = f32[1024,64]{0,1:T(8,128)} async-done(((f32[1024,256]{0,1:T(8,128)}), f32[1024,64]{0,1:T(8,128)}) %reduce-scatter.14.cloned.1.call-update) | async-done | bytes 262160 | tf_op jit(solution)/shard_map/reduce_scatter | solution.py:30
  430.4 1.6 bitcast_dynamic-update-slice_fusion
  (28 shorter events, 0.6 us)
Async XLA Ops:
  6.5 33.6 %reduce-scatter.6.cloned.1.call-start = ((), (), s32[]{:S(2)}) async-start(), calls=%async_computation.5 | async-start | bytes 1310720 | tf_op jit(solution)/shard_map/reduce_scatter | solution.py:30
  10.0 84.0 %all-gather.9.cloned.1.call-start = ((), (), s32[]{:S(2)}) async-start(), calls=%async_computation.10 | async-start | bytes 5242880 | tf_op jit(solution)/shard_map/all_gather | solution.py:27
  61.0 74.5 %reduce-scatter.8.cloned.1.call-start = ((), (), s32[]{:S(2)}) async-start(), calls=%async_computation.6 | async-start | bytes 1310720 | tf_op jit(solution)/shard_map/reduce_scatter | solution.py:30
  108.1 84.6 %all-gather.11.cloned.1.call-start = ((), (), s32[]{:S(2)}) async-start(), calls=%async_computation.11 | async-start | bytes 5242880 | tf_op jit(solution)/shard_map/all_gather | solution.py:27
  153.2 0.8 copy-start.2
  154.0 6.0 %copy-start = (bf16[1,1024,256]{2,1,0:T(8,128)(2,1)S(1)}, bf16[1,1024,256]{2,1,0:T(8,128)(2,1)}, u32[]{:S(2)}) copy-start(bf16[1,1024,256]{2,1,0:T(8,128)(2,1)} %get-tuple-element.15) | copy-start | bytes 1572868
  159.7 74.6 %reduce-scatter.10.cloned.1.call-start = ((), (), s32[]{:S(2)}) async-start(), calls=%async_computation.7 | async-start | bytes 1310720 | tf_op jit(solution)/shard_map/reduce_scatter | solution.py:30
  206.8 83.9 %all-gather.13.cloned.1.call-start = ((), (), s32[]{:S(2)}) async-start(), calls=%async_computation.12 | async-start | bytes 5242880 | tf_op jit(solution)/shard_map/all_gather | solution.py:27
  251.9 5.9 %copy-start.4 = (bf16[1024,256]{0,1:T(8,128)(2,1)}, bf16[1024,256]{0,1:T(8,128)(2,1)S(1)}, u32[]{:S(2)}) copy-start(bf16[1024,256]{0,1:T(8,128)(2,1)S(1)} %all_gather.42) | copy-start | bytes 1572868
  257.8 74.7 %reduce-scatter.12.cloned.1.call-start = ((), (), s32[]{:S(2)}) async-start(), calls=%async_computation.8 | async-start | bytes 1310720 | tf_op jit(solution)/shard_map/reduce_scatter | solution.py:30
  301.5 3.7 copy-start.3
  304.9 2.6 copy-start.5
  304.9 83.9 %all-gather.15.cloned.1.call-start = ((), (), s32[]{:S(2)}) async-start(), calls=%async_computation.13 | async-start | bytes 5242880 | tf_op jit(solution)/shard_map/all_gather | solution.py:27
  332.4 20.0 %copy-start.1 = (f32[256,1024]{1,0:T(8,128)S(1)}, f32[256,1024]{1,0:T(8,128)}, u32[]{:S(2)}) copy-start(f32[256,1024]{1,0:T(8,128)} %fusion.4) | copy-start | bytes 3145732
  355.9 74.5 %reduce-scatter.14.cloned.1.call-start = ((), (), s32[]{:S(2)}) async-start(), calls=%async_computation.9 | async-start | bytes 1310720 | tf_op jit(solution)/shard_map/reduce_scatter | solution.py:30
Sparse Core Ops, SparseCore 0:
  10.1 29.9 reduce-scatter.5
  61.2 32.7 all-gather.8
  108.2 27.2 reduce-scatter.7
  159.8 32.8 all-gather.10
  206.9 27.2 reduce-scatter.9
  257.9 32.8 all-gather.12
  305.1 27.3 reduce-scatter.11
  356.0 32.7 all-gather.14
  403.0 27.2 reduce-scatter.13
